TPU v7x, 32 devices: a whole 2x2x4 slice. The times are simulated.
32 devices in a mesh: layer: 4 (over y, x), expert: 4 (over z), dp: 2 (over core).
Axes of the slice: x: 2, y: 2, z: 4, core: 2. Of those that a mesh axis runs over, the one named last changes fastest.
Arguments:
- tokens: bfloat16 [2048, 2304], P(('expert', 'dp')), may hold values from -6 to 6
- expert_ids: int32 [2048], P(('expert', 'dp')), may hold values from 0 to 3, as said below
- slot_ids: int32 [2048], P(('expert', 'dp')), may hold values from 0 to 127, as said below
- live_mask: int32 [2048], P(('expert', 'dp')), may hold values from 0 to 1
- w_enc: bfloat16 [4, 2304, 2048], P('expert', None, 'layer'), may hold values from -0.125 to 0.125
- b_enc: float32 [4, 2048], P('expert', 'layer'), may hold values from -3 to 3
- w_dec: bfloat16 [2, 4, 2048, 2304], P(None, 'expert', 'layer'), may hold values from -0.125 to 0.125
- b_dec: float32 [2, 2304], P(None, 'layer'), may hold values from -3 to 3
- targets: bfloat16 [2, 2048, 2304], P(None, ('expert', 'dp'), 'layer'), may hold values from -6 to 6
Outputs:
- recon: bfloat16 [2, 2048, 2304], P(None, ('expert', 'dp'), 'layer')
- grad_w_enc: bfloat16 [4, 2304, 2048], P('expert', 'dp', 'layer')
- grad_b_enc: float32 [4, 2048], P('expert', ('layer', 'dp'))
- grad_w_dec: bfloat16 [2, 4, 2048, 2304], P(None, 'expert', 'layer', 'dp')
- grad_b_dec: float32 [2, 2304], P(None, 'layer')
Inputs may be any that keep to these rules, and one draw needn't show every extreme that they name: `expert_ids`: the 256 tokens of one block name any expert at most 128 times; in every draw one expert is named exactly 128 times by every block. `slot_ids`: tokens of one block that name the same expert have distinct slots.
All inputs are finite; a program needn't handle non-finite values.
Results may differ from a plain program's by a relative error of at most 0.01.
Values may be sent and summed in bfloat16 or wider, within the bound.
A program may use at most 128 MiB of HBM per device.

v0:
```python
import math
import jax
import jax.numpy as jnp
from jax import lax
from jax.sharding import PartitionSpec as P


def place_rows(values, cell_index, total_cells):
    shape = values.shape[:-2] + (total_cells, values.shape[-1])
    zero_fill = jnp.zeros(shape, values.dtype)
    return zero_fill.at[..., cell_index, :].set(values)


def local(tokens, expert_ids, slot_ids, live_mask, w_enc, b_enc, w_dec, b_dec, targets):
    n_expert = lax.axis_size("expert")
    n_layer = lax.axis_size("layer")
    tok_rows, model_width = tokens.shape
    capacity = 2 * tok_rows // n_expert
    total_cells = n_expert * capacity
    cell_index = expert_ids * capacity + slot_ids
    quarter = model_width // n_layer
    targets_count = w_dec.shape[0]
    enc_weight = w_enc[0]
    dec_weight = w_dec[:, 0]
    outgoing = place_rows(tokens, cell_index, total_cells).reshape(n_expert, capacity, model_width)
    arrived = lax.all_to_all(outgoing, "expert", split_axis=0, concat_axis=0, tiled=True).reshape(
        total_cells, model_width
    )
    pre_act = jnp.dot(arrived, enc_weight, preferred_element_type=jnp.float32)
    pre_act = pre_act + b_enc[0][None, :]
    active = jnp.maximum(pre_act, 0.0)
    latents = (active * active).astype(jnp.bfloat16)
    partials = jnp.einsum(
        "rl,tld->trd", latents, dec_weight, preferred_element_type=jnp.float32
    ).astype(jnp.bfloat16)
    summed = lax.psum_scatter(
        lax.optimization_barrier(partials).astype(jnp.float32).astype(jnp.bfloat16),
        "layer",
        scatter_dimension=2,
        tiled=True,
    )
    outgoing_rec = summed.reshape(targets_count, n_expert, capacity, quarter)
    returned = lax.all_to_all(outgoing_rec, "expert", split_axis=1, concat_axis=1, tiled=True)
    recon_sum = returned.reshape(targets_count, total_cells, quarter)[:, cell_index, :]
    recon_full = lax.optimization_barrier(recon_sum).astype(jnp.float32) + b_dec[:, None, :]
    recon = recon_full.astype(jnp.bfloat16)
    coef = 2.0 / math.sqrt(tok_rows)
    live_wide = live_mask.astype(jnp.float32)
    error_grad = (
        coef * live_wide[None, :, None] * (recon_full - targets.astype(jnp.float32))
    ).astype(jnp.bfloat16)
    error_wide = lax.optimization_barrier(error_grad).astype(jnp.float32)
    grad_b_dec = lax.psum(jnp.sum(error_wide, axis=1), ("expert", "dp"))
    outgoing_grad = place_rows(error_grad, cell_index, total_cells).reshape(
        targets_count, n_expert, capacity, quarter
    )
    error_part = lax.all_to_all(
        outgoing_grad, "expert", split_axis=1, concat_axis=1, tiled=True
    ).reshape(targets_count, total_cells, quarter)
    segment = lax.all_gather(error_part, "layer", axis=2, tiled=True)
    block_grad = jnp.einsum("rl,trd->tld", latents, segment, preferred_element_type=jnp.float32)
    grad_lat_acc = jnp.einsum(
        "trd,tld->rl", segment, dec_weight, preferred_element_type=jnp.float32
    )
    grad_pre = (grad_lat_acc * (2.0 * active)).astype(jnp.bfloat16)
    grad_enc = jnp.einsum("rd,rl->dl", arrived, grad_pre, preferred_element_type=jnp.float32)
    grad_bias = jnp.sum(lax.optimization_barrier(grad_pre).astype(jnp.float32), axis=0)
    enc_share, dec_share, bias_share = (
        lax.psum_scatter(
            grad_enc[None].astype(jnp.bfloat16), "dp", scatter_dimension=1, tiled=True
        ).astype(jnp.float32),
        lax.psum_scatter(
            block_grad[:, None].astype(jnp.bfloat16), "dp", scatter_dimension=3, tiled=True
        ).astype(jnp.float32),
        lax.psum_scatter(
            grad_bias[None].astype(jnp.bfloat16), "dp", scatter_dimension=1, tiled=True
        ).astype(jnp.float32),
    )
    return (
        recon,
        enc_share.astype(jnp.bfloat16),
        bias_share,
        dec_share.astype(jnp.bfloat16),
        grad_b_dec,
    )


def solution(mesh):
    placed = (
        P(("expert", "dp"), None),
        P(("expert", "dp")),
        P(("expert", "dp")),
        P(("expert", "dp")),
        P("expert", None, "layer"),
        P("expert", "layer"),
        P(None, "expert", "layer", None),
        P(None, "layer"),
        P(None, ("expert", "dp"), "layer"),
    )
    return jax.shard_map(
        local,
        mesh=mesh,
        in_specs=placed,
        out_specs=(
            P(None, ("expert", "dp"), "layer"),
            P("expert", "dp", "layer"),
            P("expert", ("layer", "dp")),
            P(None, "expert", "layer", "dp"),
            P(None, "layer"),
        ),
        check_vma=False,
    )
```

profile of v0, /device:TPU:0, one launch (start us, length us, event | category | flops | bytes accessed | tf_op | source)
XLA Modules:
  0.0 428.5 jit_solution(17925462820377808188)
XLA Ops:
  7.2 0.0 copy-start
  7.2 0.0 all-reduce.3.cloned.1.call-start
  7.2 0.9 compare_select_fusion
  8.1 4.7 %scatter_custom_fusion = bf16[512,2304]{1,0:T(8,128)(2,1)} fusion(s32[256]{0:T(256)S(1)} %compare_select_fusion, bf16[256,2304]{1,0:T(8,128)(2,1)} %param.9, bf16[]{:T(256)} %constant.7.clone.1), kind=kCustom, calls=%fused_computation.24 | custom fusion | bytes 2359808 | tf_op jit(solution)/shard_map/scatter | solution.py:11
  12.8 0.0 copy-start.3
  12.8 0.0 slice-start
  12.8 60.4 %all_to_all.15 = bf16[4,128,2304]{2,1,0:T(8,128)(2,1)S(1)} all-to-all(bf16[4,128,2304]{2,1,0:T(8,128)(2,1)} %bitcast.59), channel_id=1, replica_groups=mesh['layer'=4,'expert'=4,'dp'=2] {'expert'}, dimensions={0} | all-to-all | bytes 4718592 | tf_op jit(solution)/shard_map/all_to_all | solution.py:26
  73.3 0.0 copy-start.1
  73.3 1.4 copy-done.1
  74.7 0.0 copy-done
  74.7 0.0 copy-done.3
  74.7 0.0 slice-start.1
  74.7 1.4 fusion.18
  76.1 0.0 copy-start.5
  76.1 0.9 copy-done.5
  77.0 0.0 slice-done
  77.0 0.0 slice-done.1
  77.0 4.3 %fusion = bf16[2,512,2304]{2,1,0:T(8,128)(2,1)} fusion(bf16[2,1,512,2304]{3,2,1,0:T(8,128)(2,1)S(1)} %bitcast.68, f32[512,512]{1,0:T(8,128)S(1)} %fusion.18), kind=kOutput, calls=%fused_computation.5 | convolution fusion | flops 2418802688 | bytes 10485760 | tf_op jit(solution)/shard_map/rl,tld->trd/dot_general | solution.py:33
  81.4 12.4 %copy.22 = bf16[2,512,2304]{1,0,2:T(2,128)(2,1)} copy(bf16[2,512,2304]{2,1,0:T(8,128)(2,1)} %fusion) | data formatting | bytes 9437184 | tf_op jit(solution)/shard_map/optimization_barrier | solution.py:37
  93.7 0.0 copy-start.4
  93.7 0.0 all-reduce.3.cloned.1.call-update
  93.8 0.6 copy-done.4
  94.4 0.6 dynamic-slice
  95.6 109.8 %all-reduce.3.cloned.1.call-done = bf16[2,512,2304]{1,0,2:T(2,128)(2,1)} async-done(((bf16[2,512,2304]{1,0,2:T(2,128)(2,1)}), bf16[2,512,2304]{1,0,2:T(2,128)(2,1)}) %all-reduce.3.cloned.1.call-update) | async-done | bytes 4718608
  205.4 2.1 constant_dynamic-slice_fusion
  207.5 1.6 reshape.44
  209.1 2.4 copy.23
  211.6 4.6 %all-to-all-start.1 = ((bf16[2,4,128,576]{2,3,0,1:T(8,128)(2,1)}), bf16[2,4,128,576]{2,3,0,1:T(8,128)(2,1)S(1)}, u32[]{:S(2)}, u32[]{:S(2)}) async-start(bf16[2,4,128,576]{2,3,0,1:T(8,128)(2,1)} %copy.23), calls=%async_computation.1 | async-start | bytes 2359296 | tf_op jit(solution)/shard_map/all_to_all | solution.py:43
  216.2 0.0 copy-start.2
  216.2 0.0 all-gather.2.cloned.1.call-start
  216.2 2.9 copy.25
  219.0 1.2 convert_multiply_fusion
  220.3 24.2 %all-to-all-done.1 = bf16[2,4,128,576]{2,3,0,1:T(8,128)(2,1)S(1)} async-done(((bf16[2,4,128,576]{2,3,0,1:T(8,128)(2,1)}), bf16[2,4,128,576]{2,3,0,1:T(8,128)(2,1)S(1)}, u32[]{:S(2)}, u32[]{:S(2)}) %all-to-all-start.1) | async-done | bytes 1179680 | tf_op jit(solution)/shard_map/all_to_all | solution.py:43
  244.5 3.0 copy.24
  247.5 4.2 gather_fusion
  251.7 0.0 copy-done.2
  251.7 3.3 multiply_convert_fusion
  254.9 1.7 broadcast_in_dim.8
  256.7 27.0 %scatter_fusion = bf16[2,512,576]{2,0,1:T(2,128)(2,1)} fusion(bf16[2,512,576]{2,0,1:T(2,128)(2,1)} %broadcast_in_dim.8, s32[256]{0:T(256)S(1)} %compare_select_fusion, bf16[256,2,576]{2,1,0:T(2,128)(2,1)S(1)} %bitcast.61), kind=kCustom, calls=%fused_computation.2 | custom fusion | bytes 1770496 | tf_op jit(solution)/shard_map/scatter | solution.py:11
  283.7 4.2 copy.26
  287.9 31.7 %all_to_all.16 = bf16[2,4,128,576]{2,3,0,1:T(8,128)(2,1)S(1)} all-to-all(bf16[2,4,128,576]{2,3,0,1:T(8,128)(2,1)} %copy.26), channel_id=1, replica_groups=mesh['layer'=4,'expert'=4,'dp'=2] {'expert'}, dimensions={1} | all-to-all | bytes 2359296 | tf_op jit(solution)/shard_map/all_to_all | solution.py:57
  319.5 1.1 copy_bitcast_fusion
  320.7 0.0 all-gather.2.cloned.1.call-update
  320.7 0.2 reduce-scatter.10.cloned.1.call-start
  320.9 55.0 %all-gather.2.cloned.1.call-done = bf16[2,512,2304]{1,2,0:T(8,128)(2,1)} async-done(((bf16[2,512,576]{1,2,0:T(8,128)(2,1)}), bf16[2,512,2304]{1,2,0:T(8,128)(2,1)}) %all-gather.2.cloned.1.call-update) | async-done | bytes 4718608 | tf_op jit(solution)/shard_map/all_gather | solution.py:60
  375.9 6.6 %fusion.21 = bf16[512,512]{1,0:T(8,128)(2,1)S(1)} fusion(bf16[2,512,2304]{1,2,0:T(8,128)(2,1)} %all-gather.2.cloned.1.call-done, bf16[2,1,512,2304]{3,2,1,0:T(8,128)(2,1)} %param.15, f32[512,512]{1,0:T(8,128)} %copy-done.5), kind=kOutput, calls=%fused_computation.22 | convolution fusion | flops 2416705536 | bytes 11010048 | tf_op jit(solution)/shard_map/trd,tld->rl/dot_general | solution.py:62
  382.6 0.1 reduce_sum.21
  382.7 0.8 reshape_bitcast_fusion
  383.5 0.0 reduce-scatter.10.cloned.1.call-update
  383.5 0.0 reduce-scatter.8.cloned.1.call-start
  383.5 7.4 %fusion.1 = bf16[2,1,512,2304]{2,3,0,1:T(8,128)(2,1)} fusion(bf16[2,512,2304]{1,2,0:T(8,128)(2,1)} %all-gather.2.cloned.1.call-done, f32[512,512]{1,0:T(8,128)} %copy-done.5), kind=kOutput, calls=%fused_computation.6 | convolution fusion | flops 2418802688 | bytes 10485760 | tf_op jit(solution)/shard_map/rl,trd->tld/dot_general | solution.py:61
  390.9 0.0 reduce-scatter.8.cloned.1.call-update
  390.9 0.0 reduce-scatter.6.cloned.1.call-start
  391.0 4.6 %fusion.5 = bf16[1,2304,512]{2,1,0:T(8,128)(2,1)} fusion(bf16[512,2304]{1,0:T(8,128)(2,1)} %bitcast.65, bf16[512,512]{1,0:T(8,128)(2,1)S(1)} %fusion.21), kind=kOutput, calls=%fused_computation.11 | convolution fusion | flops 1209139200 | bytes 5242880 | tf_op jit(solution)/shard_map/rd,rl->dl/dot_general | solution.py:66
  395.5 0.0 reduce-scatter.6.cloned.1.call-update
  395.6 2.9 copy.28
  398.5 0.6 convert_reduce_fusion
  399.1 17.0 %psum.7 = f32[2,576]{1,0:T(2,128)} all-reduce(f32[2,576]{1,0:T(2,128)S(1)} %convert_reduce_fusion), channel_id=1, replica_groups=mesh['layer'=4,'expert'=4,'dp'=2] {'expert','dp'}, use_global_device_ids=true, to_apply=%region_8.0 | all-reduce | flops 1152 | bytes 9216 | tf_op jit(solution)/shard_map/psum | solution.py:53
  416.1 0.0 reduce-scatter.10.cloned.1.call-done
  416.1 0.9 copy.31
  417.1 0.6 convert_element_type.79
  417.7 0.0 reduce-scatter.8.cloned.1.call-done
  417.7 4.3 %copy.29 = bf16[2,1,512,1152]{3,2,1,0:T(8,128)(2,1)} copy(bf16[2,1,512,1152]{2,3,0,1:T(8,128)(2,1)} %reduce-scatter.8.cloned.1.call-done) | data formatting | bytes 4718592
  422.0 0.0 reduce-scatter.6.cloned.1.call-done
  (2 shorter events, 0.0 us)
Async XLA Ops:
  7.2 67.5 %copy-start = (bf16[1,2304,512]{2,1,0:T(8,128)(2,1)S(1)}, bf16[1,2304,512]{2,1,0:T(8,128)(2,1)}, u32[]{:S(2)}) copy-start(bf16[1,2304,512]{2,1,0:T(8,128)(2,1)} %param.13) | copy-start | bytes 7077892
  7.2 198.3 %all-reduce.3.cloned.1.call-start = ((), (), s32[]{:S(2)}) async-start(), calls=%async_computation.10 | async-start | bytes 9437184
  12.8 61.8 %copy-start.3 = (f32[1,512]{1,0:T(1,128)S(1)}, f32[1,512]{1,0:T(1,128)}, u32[]{:S(2)}) copy-start(f32[1,512]{1,0:T(1,128)} %param.14) | copy-start | bytes 6148
  12.8 64.2 %slice-start = ((s8[4718592]{0:T(1024)(128)(4,1)}), s8[4194304]{0:T(1024)(128)(4,1)S(1)}, s32[]{:S(2)}) async-start(s8[4718592]{0:T(1024)(128)(4,1)} %bitcast.67), calls=%async_computation.11 | async-start | bytes 8388608
  73.3 1.4 copy-start.1
  74.7 2.4 slice-start.1
  76.1 1.0 copy-start.5
  93.7 0.7 copy-start.4
  211.6 33.0 %all-to-all-start.1 = ((bf16[2,4,128,576]{2,3,0,1:T(8,128)(2,1)}), bf16[2,4,128,576]{2,3,0,1:T(8,128)(2,1)S(1)}, u32[]{:S(2)}, u32[]{:S(2)}) async-start(bf16[2,4,128,576]{2,3,0,1:T(8,128)(2,1)} %copy.23), calls=%async_computation.1 | async-start | bytes 2359296 | tf_op jit(solution)/shard_map/all_to_all | solution.py:43
  216.2 35.5 %copy-start.2 = (f32[2,576]{1,0:T(2,128)S(1)}, f32[2,576]{1,0:T(2,128)}, u32[]{:S(2)}) copy-start(f32[2,576]{1,0:T(2,128)} %param.16) | copy-start | bytes 13828
  216.2 159.8 %all-gather.2.cloned.1.call-start = ((), (), s32[]{:S(2)}) async-start(), calls=%async_computation.6 | async-start | bytes 5898240 | tf_op jit(solution)/shard_map/all_gather | solution.py:60
  320.7 95.4 %reduce-scatter.10.cloned.1.call-start = ((), (), s32[]{:S(2)}) async-start(), calls=%async_computation.9 | async-start | bytes 196608
  383.5 34.2 %reduce-scatter.8.cloned.1.call-start = ((), (), s32[]{:S(2)}) async-start(), calls=%async_computation.8 | async-start | bytes 7077888 | tf_op jit(solution)/shard_map/reduce_scatter | solution.py:72
  390.9 31.0 %reduce-scatter.6.cloned.1.call-start = ((), (), s32[]{:S(2)}) async-start(), calls=%async_computation.7 | async-start | bytes 3538944 | tf_op jit(solution)/shard_map/reduce_scatter | solution.py:69
Sparse Core Ops, SparseCore 0:
  93.9 111.4 all-reduce.2
  320.8 55.0 all-gather.1
  383.6 7.5 reduce-scatter.9
  393.4 13.6 reduce-scatter.7
  409.7 11.4 reduce-scatter.5
where the time goes:
time: 430 us; the launch traced here: 429 us
  waiting for transfers between devices  189 us (44%)
  blocking collectives  109 us (25%)
  local copies, waits for them, and re-layouts  79.8 us (19%)
  matrix products  24.3 us (6%)
  between operations  14.5 us (3%)
  other arithmetic  6.69 us (2%)
  starting transfers between devices  4.94 us (1%)
    unnamed x7, waiting for transfers between devices  110 us
    all_to_all x1, blocking collectives, local(): lax.all_to_all(outgoing, 'expert', split_axis=0, concat_axis=0, tiled=True)  60.4 us
    all_gather x1, waiting for transfers between devices, local(): segment = lax.all_gather(error_part, 'layer', axis=2, tiled=True)  55 us
    scatter x2, local copies, waits for them, and re-layouts, place_rows(): return zero_fill.at[..., cell_index, :].set(values)  31.8 us
    all_to_all x1, blocking collectives, local(): lax.all_to_all(outgoing_grad, 'expert', split_axis=1, concat_axis=1, tile...  31.7 us
    all_to_all x1, waiting for transfers between devices, local(): lax.all_to_all(outgoing_rec, 'expert', split_axis=1, concat_axis=1, tiled...  24.2 us
    unnamed x23, local copies, waits for them, and re-layouts  17.5 us
    psum x1, blocking collectives, local(): grad_b_dec = lax.psum(jnp.sum(error_wide, axis=1), ('expert', 'dp'))  17 us
  transfers between devices with their start and end apart: 6, of which 3 were waited for; matrix products, arithmetic and copies ran while one was open for 6% of the time, Pallas kernels for 0%

commit v1 on v0

--- a/solution.py
+++ b/solution.py
@@ -57,7 +57,7 @@
     error_part = lax.all_to_all(
         outgoing_grad, "expert", split_axis=1, concat_axis=1, tiled=True
     ).reshape(targets_count, total_cells, quarter)
-    segment = lax.all_gather(error_part, "layer", axis=2, tiled=True)
+    segment = jnp.concatenate(lax.all_gather(error_part, "layer"), axis=2)
     block_grad = jnp.einsum("rl,trd->tld", latents, segment, preferred_element_type=jnp.float32)
     grad_lat_acc = jnp.einsum(
         "trd,tld->rl", segment, dec_weight, preferred_element_type=jnp.float32

time: 430 us -> 406 us (0.944)
  local copies, waits for them, and re-layouts: 79.8 us -> 58.5 us
    scatter x2, local copies, waits for them, and re-layouts: 31.8 us -> 11.9 us  [place_rows(): return zero_fill.at[..., cell_index, :].set(values)]
    unnamed x23 -> x35, local copies, waits for them, and re-layouts: 17.5 us -> 18.5 us
  transfers between devices with their start and end apart: 6 -> 6, of which waited for: 3 -> 3; matrix products, arithmetic and copies ran while one was open for 6% -> 5% of each run, Pallas kernels for 0% -> 0%
where the time goes in v1:
time: 406 us; the launch traced here: 405 us
  waiting for transfers between devices  192 us (47%)
  blocking collectives  108 us (27%)
  local copies, waits for them, and re-layouts  58.5 us (14%)
  matrix products  21.9 us (5%)
  between operations  14.6 us (4%)
  starting transfers between devices  4.9 us (1%)
  other arithmetic  4.5 us (1%)
    unnamed x7, waiting for transfers between devices  110 us
    all_to_all x1, blocking collectives, local(): lax.all_to_all(outgoing, 'expert', split_axis=0, concat_axis=0, tiled=True)  60.4 us
    all_gather x1, waiting for transfers between devices, local(): segment = jnp.concatenate(lax.all_gather(error_part, 'layer'), axis=2)  55.2 us
    all_to_all x1, blocking collectives, local(): lax.all_to_all(outgoing_grad, 'expert', split_axis=1, concat_axis=1, tile...  30.5 us
    all_to_all x1, waiting for transfers between devices, local(): lax.all_to_all(outgoing_rec, 'expert', split_axis=1, concat_axis=1, tiled...  27.2 us
    unnamed x35, local copies, waits for them, and re-layouts  18.5 us
    psum x1, blocking collectives, local(): grad_b_dec = lax.psum(jnp.sum(error_wide, axis=1), ('expert', 'dp'))  17 us
    optimization_barrier x1, local copies, waits for them, and re-layouts, local(): lax.optimization_barrier(partials).astype(jnp.float32).astype(jnp.bfloat16)  12.4 us
  transfers between devices with their start and end apart: 6, of which 3 were waited for; matrix products, arithmetic and copies ran while one was open for 5% of the time, Pallas kernels for 0%

profile of v1, /device:TPU:0, one launch (start us, length us, event | category | flops | bytes accessed | tf_op | source)
XLA Modules:
  0.0 404.7 jit_solution(15275040843577560385)
XLA Ops:
  7.2 0.0 copy-start
  7.2 0.0 all-reduce.3.cloned.1.call-start
  7.2 0.9 compare_select_fusion
  8.1 4.7 %scatter_custom_fusion = bf16[512,2304]{1,0:T(8,128)(2,1)} fusion(s32[256]{0:T(256)S(1)} %compare_select_fusion, bf16[256,2304]{1,0:T(8,128)(2,1)} %param.9, bf16[]{:T(256)} %constant.7.clone.1), kind=kCustom, calls=%fused_computation.23 | custom fusion | bytes 2359808 | tf_op jit(solution)/shard_map/scatter | solution.py:11
  12.8 60.4 %all_to_all.15 = bf16[4,128,2304]{2,1,0:T(8,128)(2,1)S(1)} all-to-all(bf16[4,128,2304]{2,1,0:T(8,128)(2,1)} %bitcast.59), channel_id=1, replica_groups=mesh['layer'=4,'expert'=4,'dp'=2] {'expert'}, dimensions={0} | all-to-all | bytes 4718592 | tf_op jit(solution)/shard_map/all_to_all | solution.py:26
  73.3 1.4 copy-done.4
  74.7 0.0 copy-done
  74.7 0.0 copy-done.8
  74.7 1.4 fusion.18
  76.1 0.0 copy-start.10
  76.1 0.9 copy-done.10
  77.0 0.0 slice-done
  77.0 0.0 slice-done.1
  77.0 4.3 %fusion = bf16[2,512,2304]{2,1,0:T(8,128)(2,1)} fusion(bf16[2,1,512,2304]{3,2,1,0:T(8,128)(2,1)S(1)} %bitcast.70, f32[512,512]{1,0:T(8,128)S(1)} %fusion.18), kind=kOutput, calls=%fused_computation.5 | convolution fusion | flops 2418802688 | bytes 10485760 | tf_op jit(solution)/shard_map/rl,tld->trd/dot_general | solution.py:33
  81.3 12.4 %copy.25 = bf16[2,512,2304]{1,0,2:T(2,128)(2,1)} copy(bf16[2,512,2304]{2,1,0:T(8,128)(2,1)} %fusion) | data formatting | bytes 9437184 | tf_op jit(solution)/shard_map/optimization_barrier | solution.py:37
  93.7 0.0 all-reduce.3.cloned.1.call-update
  93.8 0.6 copy-done.9
  94.4 0.6 dynamic-slice
  95.6 109.8 %all-reduce.3.cloned.1.call-done = bf16[2,512,2304]{1,0,2:T(2,128)(2,1)} async-done(((bf16[2,512,2304]{1,0,2:T(2,128)(2,1)}), bf16[2,512,2304]{1,0,2:T(2,128)(2,1)}) %all-reduce.3.cloned.1.call-update) | async-done | bytes 4718608
  205.4 2.1 constant_dynamic-slice_fusion
  207.5 0.8 reshape.47
  208.3 0.0 copy-start.5
  208.3 1.2 copy.26
  209.5 4.7 %all-to-all-start.1 = ((bf16[2,4,128,576]{2,3,0,1:T(8,128)(2,1)}), bf16[2,4,128,576]{2,3,0,1:T(8,128)(2,1)S(1)}, u32[]{:S(2)}, u32[]{:S(2)}) async-start(bf16[2,4,128,576]{2,3,0,1:T(8,128)(2,1)} %copy.26), calls=%async_computation.1 | async-start | bytes 2359296 | tf_op jit(solution)/shard_map/all_to_all | solution.py:43
  214.3 0.0 all-gather.2.cloned.1.call-start
  214.3 0.0 copy-done.5
  214.3 1.1 copy.28
  215.4 0.0 copy-done.7
  215.4 27.2 %all-to-all-done.1 = bf16[2,4,128,576]{2,3,0,1:T(8,128)(2,1)S(1)} async-done(((bf16[2,4,128,576]{2,3,0,1:T(8,128)(2,1)}), bf16[2,4,128,576]{2,3,0,1:T(8,128)(2,1)S(1)}, u32[]{:S(2)}, u32[]{:S(2)}) %all-to-all-start.1) | async-done | bytes 1179680 | tf_op jit(solution)/shard_map/all_to_all | solution.py:43
  242.6 2.9 copy.27
  245.5 3.4 gather_fusion
  248.9 0.0 copy-done.6
  248.9 2.3 multiply_convert_fusion
  251.3 0.7 broadcast_in_dim.8
  251.9 7.1 %scatter_fusion = bf16[2,512,576]{2,0,1:T(2,128)(2,1)S(1)} fusion(bf16[2,512,576]{2,0,1:T(2,128)(2,1)S(1)} %broadcast_in_dim.8, s32[256]{0:T(256)S(1)} %compare_select_fusion, bf16[256,2,576]{2,1,0:T(2,128)(2,1)S(1)} %bitcast.61), kind=kCustom, calls=%fused_computation.2 | custom fusion | bytes 1770496 | tf_op jit(solution)/shard_map/scatter | solution.py:11
  259.1 2.0 copy.29
  261.0 30.5 %all_to_all.16 = bf16[2,4,128,576]{2,3,0,1:T(8,128)(2,1)S(1)} all-to-all(bf16[2,4,128,576]{2,3,0,1:T(8,128)(2,1)S(1)} %copy.29), channel_id=1, replica_groups=mesh['layer'=4,'expert'=4,'dp'=2] {'expert'}, dimensions={1} | all-to-all | bytes 2359296 | tf_op jit(solution)/shard_map/all_to_all | solution.py:57
  291.6 0.9 copy.30
  292.5 1.3 all_gather_reshape.3
  293.8 0.0 all-gather.2.cloned.1.call-update
  293.8 0.0 copy-start.11
  293.8 0.0 reduce-scatter.10.cloned.1.call-start
  293.9 55.2 %all-gather.2.cloned.1.call-done = bf16[4,2,512,576]{2,3,1,0:T(8,128)(2,1)} async-done(((bf16[1,2,512,576]{2,3,1,0:T(8,128)(2,1)}), bf16[4,2,512,576]{2,3,1,0:T(8,128)(2,1)}) %all-gather.2.cloned.1.call-update) | async-done | bytes 4718608 | tf_op jit(solution)/shard_map/all_gather | solution.py:60
  349.0 2.6 copy.31
  351.7 0.0 copy-start.2
  351.7 2.2 copy-done.2
  353.8 0.0 copy-done.11
  353.8 5.0 %fusion.21 = bf16[512,512]{1,0:T(8,128)(2,1)S(1)} fusion(bf16[2,512,2304]{1,2,0:T(8,128)(2,1)S(1)} %bitcast.62, bf16[2,1,512,2304]{3,2,1,0:T(8,128)(2,1)} %param.15, f32[512,512]{1,0:T(8,128)S(1)} %copy-done.11), kind=kOutput, calls=%fused_computation.22 | convolution fusion | flops 2416705536 | bytes 11010048 | tf_op jit(solution)/shard_map/trd,tld->rl/dot_general | solution.py:62
  358.8 0.1 reduce_sum.21
  358.9 0.8 reshape_bitcast_fusion
  359.7 0.0 reduce-scatter.10.cloned.1.call-update
  359.8 0.0 reduce-scatter.8.cloned.1.call-start
  359.8 6.6 %fusion.1 = bf16[2,1,512,2304]{2,3,0,1:T(8,128)(2,1)} fusion(bf16[2,512,2304]{1,2,0:T(8,128)(2,1)} %bitcast.63, f32[512,512]{1,0:T(8,128)S(1)} %copy-done.11), kind=kOutput, calls=%fused_computation.6 | convolution fusion | flops 2418802688 | bytes 10485760 | tf_op jit(solution)/shard_map/rl,trd->tld/dot_general | solution.py:61
  366.4 0.0 reduce-scatter.8.cloned.1.call-update
  366.5 0.0 reduce-scatter.6.cloned.1.call-start
  366.5 4.6 %fusion.5 = bf16[1,2304,512]{2,1,0:T(8,128)(2,1)} fusion(bf16[512,2304]{1,0:T(8,128)(2,1)} %bitcast.67, bf16[512,512]{1,0:T(8,128)(2,1)S(1)} %fusion.21), kind=kOutput, calls=%fused_computation.11 | convolution fusion | flops 1209139200 | bytes 5242880 | tf_op jit(solution)/shard_map/rd,rl->dl/dot_general | solution.py:66
  371.1 0.0 reduce-scatter.6.cloned.1.call-update
  371.1 1.1 copy-done.3
  372.2 1.9 copy.33
  374.1 0.6 convert_reduce_fusion
  374.7 17.0 %psum.7 = f32[2,576]{1,0:T(2,128)} all-reduce(f32[2,576]{1,0:T(2,128)S(1)} %convert_reduce_fusion), channel_id=1, replica_groups=mesh['layer'=4,'expert'=4,'dp'=2] {'expert','dp'}, use_global_device_ids=true, to_apply=%region_8.0 | all-reduce | flops 1152 | bytes 9216 | tf_op jit(solution)/shard_map/psum | solution.py:53
  391.8 0.9 copy.37
  392.7 0.6 convert_element_type.79
  393.3 4.9 %copy.34 = bf16[2,1,512,1152]{3,2,1,0:T(8,128)(2,1)} copy(bf16[2,1,512,1152]{2,3,0,1:T(8,128)(2,1)} %reduce-scatter.8.cloned.1.call-done) | data formatting | bytes 4718592
  (16 shorter events, 0.0 us)
Async XLA Ops:
  7.2 67.5 %copy-start = (bf16[1,2304,512]{2,1,0:T(8,128)(2,1)S(1)}, bf16[1,2304,512]{2,1,0:T(8,128)(2,1)}, u32[]{:S(2)}) copy-start(bf16[1,2304,512]{2,1,0:T(8,128)(2,1)} %param.13) | copy-start | bytes 7077892
  7.2 198.2 %all-reduce.3.cloned.1.call-start = ((), (), s32[]{:S(2)}) async-start(), calls=%async_computation.10 | async-start | bytes 9437184
  12.8 61.8 %copy-start.8 = (f32[1,512]{1,0:T(1,128)S(1)}, f32[1,512]{1,0:T(1,128)}, u32[]{:S(2)}) copy-start(f32[1,512]{1,0:T(1,128)} %param.14) | copy-start | bytes 6148
  12.8 64.2 %slice-start = ((s8[4718592]{0:T(1024)(128)(4,1)}), s8[4194304]{0:T(1024)(128)(4,1)S(1)}, s32[]{:S(2)}) async-start(s8[4718592]{0:T(1024)(128)(4,1)} %bitcast.69), calls=%async_computation.11 | async-start | bytes 8388608
  73.3 1.4 copy-start.4
  74.7 2.4 slice-start.1
  76.1 1.0 copy-start.10
  93.7 0.7 copy-start.9
  208.3 6.0 %copy-start.5 = (bf16[2,256,576]{1,2,0:T(8,128)(2,1)S(1)}, bf16[2,256,576]{1,2,0:T(8,128)(2,1)}, u32[]{:S(2)}) copy-start(bf16[2,256,576]{1,2,0:T(8,128)(2,1)} %param.17) | copy-start | bytes 1769476
  209.5 5.8 %copy-start.7 = (s32[256]{0:T(256)S(1)}, s32[256]{0:T(256)}, u32[]{:S(2)}) copy-start(s32[256]{0:T(256)} %param.12) | copy-start | bytes 3076
  209.5 33.1 %all-to-all-start.1 = ((bf16[2,4,128,576]{2,3,0,1:T(8,128)(2,1)}), bf16[2,4,128,576]{2,3,0,1:T(8,128)(2,1)S(1)}, u32[]{:S(2)}, u32[]{:S(2)}) async-start(bf16[2,4,128,576]{2,3,0,1:T(8,128)(2,1)} %copy.26), calls=%async_computation.1 | async-start | bytes 2359296 | tf_op jit(solution)/shard_map/all_to_all | solution.py:43
  214.3 34.7 %copy-start.6 = (f32[2,576]{1,0:T(2,128)S(1)}, f32[2,576]{1,0:T(2,128)}, u32[]{:S(2)}) copy-start(f32[2,576]{1,0:T(2,128)} %param.16) | copy-start | bytes 13828
  214.3 134.8 %all-gather.2.cloned.1.call-start = ((), (), s32[]{:S(2)}) async-start(), calls=%async_computation.6 | async-start | bytes 5898240 | tf_op jit(solution)/shard_map/all_gather | solution.py:60
  293.8 60.0 %copy-start.11 = (f32[512,512]{1,0:T(8,128)S(1)}, f32[512,512]{1,0:T(8,128)}, u32[]{:S(2)}) copy-start(f32[512,512]{1,0:T(8,128)} %copy-done.10) | copy-start | bytes 3145732
  293.8 98.0 %reduce-scatter.10.cloned.1.call-start = ((), (), s32[]{:S(2)}) async-start(), calls=%async_computation.9 | async-start | bytes 196608
  351.7 2.2 copy-start.2
  359.8 33.5 %reduce-scatter.8.cloned.1.call-start = ((), (), s32[]{:S(2)}) async-start(), calls=%async_computation.8 | async-start | bytes 7077888 | tf_op jit(solution)/shard_map/reduce_scatter | solution.py:72
  366.5 31.7 %reduce-scatter.6.cloned.1.call-start = ((), (), s32[]{:S(2)}) async-start(), calls=%async_computation.7 | async-start | bytes 3538944 | tf_op jit(solution)/shard_map/reduce_scatter | solution.py:69
  371.1 1.1 copy-start.3
  392.7 5.5 %copy-start.1 = (bf16[1,2304,512]{2,1,0:T(8,128)(2,1)S(1)}, bf16[1,2304,512]{2,1,0:T(8,128)(2,1)}, u32[]{:S(2)}) copy-start(bf16[1,2304,512]{2,1,0:T(8,128)(2,1)} %param.13) | copy-start | bytes 7077892
Sparse Core Ops, SparseCore 0:
  93.9 111.4 all-reduce.2
  293.9 55.0 all-gather.1
  359.9 7.5 reduce-scatter.9
  369.7 13.6 reduce-scatter.7
  386.0 11.4 reduce-scatter.5
